TPU v7x, 256 devices: a whole 4x4x8 slice. The times are simulated.
256 devices in a mesh: row: 32 (over z, y_hi, core), col: 8 (over y_lo, x).
Axes of the slice: x: 4, y: 4 (y_hi: 2, y_lo: 2; y = y_hi * 2 + y_lo), z: 8, core: 2. Of those that a mesh axis runs over, the one named last changes fastest.
Arguments:
- p_vals: float32 [128, 16, 128, 128], P('row', 'col'), may hold values from -2 to 2
- p_cols: int32 [128, 16], P('row'), may hold values from 0 to 127, as said below
- out_cols: int32 [128, 16], P('row'), may hold values from 0 to 127, as said below
Outputs:
- c_vals: float32 [128, 16, 128, 128], P('row', 'col')
Inputs may be any that keep to these rules, and one draw needn't show every extreme that they name: Block column indices; p_cols[i, s] // 4 equals (i // 4 + s // 2 - t) mod 32 for some t of 0, 1, 2, 3. `out_cols`: each output block column is p_cols[p_cols[i, s], s2] for some slots s and s2.
All inputs are finite; a program needn't handle non-finite values.
Results may differ from a plain program's by a relative error of at most 0.0003.
Values sent between devices are 32-bit elements; how exact they have to be, the bound alone decides.
A program may use at most 64 MiB of HBM per device.

v0:
```python
import jax
import jax.numpy as jnp
from jax import lax
from jax.sharding import PartitionSpec as P


def from_behind(block, axis, distance):
    devices = range(lax.axis_size(axis))
    route = [((i - distance) % len(devices), i) for i in devices]
    return lax.ppermute(block, axis, route)


def on_device(p_vals, p_cols, out_cols):
    rows = p_vals.shape[0]
    slots_dev = p_vals.shape[1]
    nrow = lax.axis_size("row")
    ncol = lax.axis_size("col")
    row_at = lax.axis_index("row")
    col_at = lax.axis_index("col")
    own_cols = lax.dynamic_slice_in_dim(p_cols, col_at * slots_dev, slots_dev, 1)
    panel_vals = lax.all_gather(p_vals, "col", axis=1, tiled=True)
    panel_cols = p_cols
    for bit in range((ncol - 1).bit_length()):
        moved = from_behind((panel_vals, panel_cols), "row", nrow - (1 << bit))
        taken = col_at >> bit & 1 == 1
        panel_vals = jnp.where(taken, moved[0], panel_vals)
        panel_cols = jnp.where(taken, moved[1], panel_cols)
    local_ids = jnp.arange(rows, dtype=jnp.int32)
    block = p_vals.shape[2]
    total = jnp.zeros((rows, out_cols.shape[1], block, block), jnp.float32)
    for step in range(3):
        if step > 0:
            panel_vals, panel_cols = from_behind((panel_vals, panel_cols), "row", 1)
        group_now = (row_at + col_at - step) % nrow
        local_k = own_cols - group_now * rows
        select = (local_k[:, :, None] == local_ids[None, None, :]).astype(jnp.float32)
        match = (out_cols[:, :, None, None] == panel_cols[None, None, :, :]).astype(jnp.float32)
        weights = jnp.einsum("isl,iolt->isolt", select, match)
        mixed = jnp.einsum(
            "isolt,ltab->isoab", weights, panel_vals, precision=lax.Precision.HIGHEST
        )
        total = total + jnp.einsum(
            "isab,isobc->ioac", p_vals, mixed, precision=lax.Precision.HIGHEST
        )
    return lax.psum_scatter(total, "col", scatter_dimension=1, tiled=True)


def solution(mesh):
    placed = (P("row", "col", None, None), P("row", None), P("row", None))
    return jax.shard_map(
        on_device,
        mesh=mesh,
        in_specs=placed,
        out_specs=P("row", "col", None, None),
        check_vma=False,
    )
```

profile of v0, /device:TPU:1, one launch (start us, length us, event | category | flops | bytes accessed | tf_op | source)
XLA Modules:
  0.0 630.7 jit_solution(2252612988769538161)
XLA Ops:
  6.5 0.0 all-gather.2.cloned.1.call-start
  6.5 1.9 copy.18
  8.4 0.0 all-gather.2.cloned.1.call-update
  8.4 0.0 all-reduce.3.cloned.1.call-start
  8.5 59.3 %all-gather.2.cloned.1.call-done = f32[4,16,128,128]{3,2,0,1:T(8,128)} async-done(((f32[4,2,128,128]{3,2,0,1:T(8,128)}), f32[4,16,128,128]{3,2,0,1:T(8,128)}) %all-gather.2.cloned.1.call-update) | async-done | bytes 4194320 | tf_op jit(solution)/shard_map/all_gather | solution.py:21
  67.8 6.6 %copy.19 = f32[4,16,128,128]{3,1,0,2:T(8,128)} copy(f32[4,16,128,128]{3,2,0,1:T(8,128)} %all-gather.2.cloned.1.call-done) | data formatting | bytes 8388608 | tf_op jit(solution)/shard_map/all_gather | solution.py:21
  74.4 0.8 collective-permute-start.3
  75.3 48.9 %collective-permute-done.3 = f32[4,16,128,128]{3,1,0,2:T(8,128)} collective-permute-done((f32[4,16,128,128]{3,1,0,2:T(8,128)}, f32[4,16,128,128]{3,1,0,2:T(8,128)}, u32[]{:S(2)}, u32[]{:S(2)}) %collective-permute-start.3) | collective-permute-done | bytes 4194336 | tf_op jit(solution)/shard_map/ppermute | solution.py:10
  124.2 6.6 %broadcast_select_fusion = f32[4,16,128,128]{3,1,0,2:T(8,128)} fusion(f32[4,16,128,128]{3,1,0,2:T(8,128)} %collective-permute-done.3, pred[]{:T(512)S(6)} %eq.45, f32[4,16,128,128]{3,2,0,1:T(8,128)} %all-gather.2.cloned.1.call-done), kind=kLoop, calls=%fused_computation.18 | loop fusion | flops 1048576 | bytes 12582913 | tf_op jit(solution)/shard_map/jit(_where)/select_n | solution.py:26
  130.8 7.3 %collective-permute-start.4 = (f32[4,16,128,128]{3,1,0,2:T(8,128)}, f32[4,16,128,128]{3,1,0,2:T(8,128)}, u32[]{:S(2)}, u32[]{:S(2)}) collective-permute-start(f32[4,16,128,128]{3,1,0,2:T(8,128)} %broadcast_select_fusion), channel_id=1, source_target_pairs={{16,0},{24,8},{32,16},{40,24},{48,32},{56,40},{64,48},{72,56},{80,... | collective-permute-start | bytes 12582920 | tf_op jit(solution)/shard_map/ppermute | solution.py:10
  138.1 86.6 %collective-permute-done.4 = f32[4,16,128,128]{3,1,0,2:T(8,128)} collective-permute-done((f32[4,16,128,128]{3,1,0,2:T(8,128)}, f32[4,16,128,128]{3,1,0,2:T(8,128)}, u32[]{:S(2)}, u32[]{:S(2)}) %collective-permute-start.4) | collective-permute-done | bytes 4194336 | tf_op jit(solution)/shard_map/ppermute | solution.py:10
  224.7 5.5 broadcast_select_fusion.1
  230.2 4.0 collective-permute-start.5
  234.2 0.0 copy-start.2
  234.2 0.0 copy-start.3
  234.2 90.4 %collective-permute-done.5 = f32[4,16,128,128]{3,1,0,2:T(8,128)} collective-permute-done((f32[4,16,128,128]{3,1,0,2:T(8,128)}, f32[4,16,128,128]{3,1,0,2:T(8,128)}, u32[]{:S(2)}, u32[]{:S(2)}) %collective-permute-start.5) | collective-permute-done | bytes 4194336 | tf_op jit(solution)/shard_map/ppermute | solution.py:10
  324.6 3.1 broadcast_select_fusion.2
  327.8 0.0 copy-start
  327.8 2.0 copy-done
  329.8 0.0 collective-permute-start.7
  329.8 45.4 %collective-permute-done.7 = f32[4,16,128,128]{3,1,0,2:T(8,128)} collective-permute-done((f32[4,16,128,128]{3,1,0,2:T(8,128)S(1)}, f32[4,16,128,128]{3,1,0,2:T(8,128)}, u32[]{:S(2)}, u32[]{:S(2)}) %collective-permute-start.7) | collective-permute-done | bytes 4194336 | tf_op jit(solution)/shard_map/ppermute | solution.py:10
  375.2 4.1 collective-permute-start.9
  379.3 0.0 copy-done.2
  379.3 3.0 collective-permute-start
  382.3 1.8 collective-permute-done
  384.0 9.9 %collective-permute-start.1 = (s32[4,16]{1,0:T(4,128)S(1)}, s32[4,16]{1,0:T(4,128)S(1)}, u32[]{:S(2)}, u32[]{:S(2)}) collective-permute-start(s32[4,16]{1,0:T(4,128)S(1)} %broadcast_select_fusion.3), channel_id=1, source_target_pairs={{16,0},{24,8},{32,16},{40,24},{48,32},{56,40},{64,48},{72,56},{80,... | collective-permute-start | bytes 776 | tf_op jit(solution)/shard_map/ppermute | solution.py:10
  394.0 0.1 dynamic-slice_subtract_fusion.2
  394.0 0.7 collective-permute-done.1
  394.7 1.1 collective-permute-start.2
  395.8 1.8 collective-permute-done.2
  397.5 0.2 collective-permute-start.6
  397.7 0.1 fusion.37
  397.8 27.3 %collective-permute-done.6 = s32[4,16]{1,0:T(4,128)S(1)} collective-permute-done((s32[4,16]{1,0:T(4,128)S(1)}, s32[4,16]{1,0:T(4,128)S(1)}, u32[]{:S(2)}, u32[]{:S(2)}) %collective-permute-start.6) | collective-permute-done | bytes 288 | tf_op jit(solution)/shard_map/ppermute | solution.py:10
  425.1 4.0 collective-permute-start.8
  429.1 0.1 fusion.36
  429.2 5.4 collective-permute-done.8
  434.6 0.0 copy-done.3
  434.6 0.1 convert_bitcast_fusion.2
  434.7 9.0 %fusion.13 = f32[4,2,16,128,128]{4,2,3,1,0:T(8,128)S(1)} fusion(f32[4,16,128,128]{3,1,0,2:T(8,128)} %copy-done, f32[4,4,2]{2,1,0:T(4,128)S(1)} %convert_bitcast_fusion.3, f32[4,4,16,16]{3,2,1,0:T(8,128)S(1)} %get-tuple-element.5), kind=kOutput, calls=%fused_computation.15 | convolution fusion | flops 1610620928 | bytes 12599424 | tf_op jit(solution)/shard_map/isolt,ltab->isoab/dot_general | solution.py:39
  443.8 0.0 copy-start.1
  443.8 9.5 %fusion.16 = f32[4,2,16,128,128]{4,2,3,1,0:T(8,128)S(1)} fusion(f32[4,16,128,128]{3,1,0,2:T(8,128)} %collective-permute-done.7, f32[4,4,2]{1,2,0:T(2,128)S(1)} %fusion.36, f32[4,4,16,16]{3,2,1,0:T(8,128)S(1)} %get-tuple-element.6), kind=kOutput, calls=%fused_computation.16 | convolution fusion | flops 1610620928 | bytes 12599424 | tf_op jit(solution)/shard_map/isolt,ltab->isoab/dot_general | solution.py:39
  453.3 0.0 copy-done.1
  453.3 16.1 %fusion.2 = f32[4,16,128,128,1]{3,2,4,1,0:T(8,128)S(1)} fusion(f32[4,2,16,128,128]{4,2,3,1,0:T(8,128)S(1)} %fusion.16, f32[4,2,128,128]{3,2,1,0:T(8,128)S(1)} %copy-done.1), kind=kOutput, calls=%fused_computation.2 | convolution fusion | flops 3221225472 | bytes 13107200 | tf_op jit(solution)/shard_map/isab,isobc->ioac/dot_general | solution.py:42
  469.4 0.0 collective-permute-done.9
  469.4 9.0 %fusion.19 = f32[4,2,16,128,128]{4,2,3,1,0:T(8,128)S(1)} fusion(f32[4,16,128,128]{3,1,0,2:T(8,128)} %collective-permute-done.9, f32[4,4,2]{1,2,0:T(2,128)S(1)} %fusion.37, f32[4,4,16,16]{3,2,1,0:T(8,128)S(1)} %get-tuple-element.7), kind=kOutput, calls=%fused_computation.17 | convolution fusion | flops 1610620928 | bytes 12599424 | tf_op jit(solution)/shard_map/isolt,ltab->isoab/dot_general | solution.py:39
  478.5 15.7 %fusion = f32[4,16,128,128,1]{3,2,4,1,0:T(8,128)S(1)} fusion(f32[4,2,16,128,128]{4,2,3,1,0:T(8,128)S(1)} %fusion.19, f32[4,2,128,128]{3,2,1,0:T(8,128)S(1)} %copy-done.1), kind=kOutput, calls=%fused_computation | convolution fusion | flops 3221225472 | bytes 13107200 | tf_op jit(solution)/shard_map/isab,isobc->ioac/dot_general | solution.py:42
  494.2 15.7 %fusion.12 = f32[4,16,128,128]{2,3,1,0:T(8,128)} fusion(f32[4,16,128,128,1]{3,2,4,1,0:T(8,128)S(1)} %fusion, f32[4,16,128,128,1]{3,2,4,1,0:T(8,128)S(1)} %fusion.2, f32[4,2,16,128,128]{4,2,3,1,0:T(8,128)S(1)} %fusion.13, f32[4,2,128,128]{3,2,1,0:T(8,128)S(1)} %copy-done.1), kind=kOutput, calls=%fused_computation.13 | convolution fusion | flops 3223322624 | bytes 21495808 | tf_op jit(solution)/shard_map/isab,isobc->ioac/dot_general | solution.py:42
  509.9 0.0 copy-start.4
  509.9 0.0 all-reduce.3.cloned.1.call-update
  509.9 0.6 copy-done.4
  510.6 0.6 dynamic-slice
  511.8 109.6 %all-reduce.3.cloned.1.call-done = f32[4,16,128,128]{2,3,1,0:T(8,128)} async-done(((f32[4,16,128,128]{2,3,1,0:T(8,128)}), f32[4,16,128,128]{2,3,1,0:T(8,128)}) %all-reduce.3.cloned.1.call-update) | async-done | bytes 4194320
  621.4 1.1 constant_dynamic-slice_fusion
  622.4 1.0 copy.25
  (4 shorter events, 0.0 us)
Async XLA Ops:
  6.5 61.3 %all-gather.2.cloned.1.call-start = ((), (), s32[]{:S(2)}) async-start(), calls=%async_computation | async-start | bytes 4718592 | tf_op jit(solution)/shard_map/all_gather | solution.py:21
  8.4 612.9 %all-reduce.3.cloned.1.call-start = ((), (), s32[]{:S(2)}) async-start(), calls=%async_computation.1 | async-start | bytes 8388608
  74.4 49.8 %collective-permute-start.3 = (f32[4,16,128,128]{3,1,0,2:T(8,128)}, f32[4,16,128,128]{3,1,0,2:T(8,128)}, u32[]{:S(2)}, u32[]{:S(2)}) collective-permute-start(f32[4,16,128,128]{3,1,0,2:T(8,128)} %copy.19), channel_id=1, source_target_pairs={{8,0},{16,8},{24,16},{32,24},{40,32},{48,40},{56,48},{64,56},{72,6... | collective-permute-start | bytes 12582920 | tf_op jit(solution)/shard_map/ppermute | solution.py:10
  130.8 93.9 %collective-permute-start.4 = (f32[4,16,128,128]{3,1,0,2:T(8,128)}, f32[4,16,128,128]{3,1,0,2:T(8,128)}, u32[]{:S(2)}, u32[]{:S(2)}) collective-permute-start(f32[4,16,128,128]{3,1,0,2:T(8,128)} %broadcast_select_fusion), channel_id=1, source_target_pairs={{16,0},{24,8},{32,16},{40,24},{48,32},{56,40},{64,48},{72,56},{80,... | collective-permute-start | bytes 12582920 | tf_op jit(solution)/shard_map/ppermute | solution.py:10
  230.2 94.4 %collective-permute-start.5 = (f32[4,16,128,128]{3,1,0,2:T(8,128)}, f32[4,16,128,128]{3,1,0,2:T(8,128)}, u32[]{:S(2)}, u32[]{:S(2)}) collective-permute-start(f32[4,16,128,128]{3,1,0,2:T(8,128)} %broadcast_select_fusion.1), channel_id=1, source_target_pairs={{32,0},{40,8},{48,16},{56,24},{64,32},{72,40},{80,48},{88,56},{96,... | collective-permute-start | bytes 12582920 | tf_op jit(solution)/shard_map/ppermute | solution.py:10
  234.2 145.1 %copy-start.2 = (s32[4,16]{1,0:T(4,128)S(1)}, s32[4,16]{1,0:T(4,128)}, u32[]{:S(2)}) copy-start(s32[4,16]{1,0:T(4,128)} %param.4) | copy-start | bytes 772
  234.2 200.4 %copy-start.3 = (s32[4,16]{1,0:T(4,128)S(1)}, s32[4,16]{1,0:T(4,128)}, u32[]{:S(2)}) copy-start(s32[4,16]{1,0:T(4,128)} %param.5) | copy-start | bytes 772
  327.8 2.0 copy-start
  329.8 45.5 %collective-permute-start.7 = (f32[4,16,128,128]{3,1,0,2:T(8,128)S(1)}, f32[4,16,128,128]{3,1,0,2:T(8,128)}, u32[]{:S(2)}, u32[]{:S(2)}) collective-permute-start(f32[4,16,128,128]{3,1,0,2:T(8,128)S(1)} %broadcast_select_fusion.2), channel_id=1, source_target_pairs={{248,0},{0,8},{8,16},{16,24},{24,32},{32,40},{40,48},{48,56},{56,6... | collective-permute-start | bytes 12582920 | tf_op jit(solution)/shard_map/ppermute | solution.py:10
  375.2 94.2 %collective-permute-start.9 = (f32[4,16,128,128]{3,1,0,2:T(8,128)}, f32[4,16,128,128]{3,1,0,2:T(8,128)}, u32[]{:S(2)}, u32[]{:S(2)}) collective-permute-start(f32[4,16,128,128]{3,1,0,2:T(8,128)} %collective-permute-done.7), channel_id=1, source_target_pairs={{248,0},{0,8},{8,16},{16,24},{24,32},{32,40},{40,48},{48,56},{56,6... | collective-permute-start | bytes 12582920 | tf_op jit(solution)/shard_map/ppermute | solution.py:10
  379.3 4.7 collective-permute-start
  384.0 10.7 %collective-permute-start.1 = (s32[4,16]{1,0:T(4,128)S(1)}, s32[4,16]{1,0:T(4,128)S(1)}, u32[]{:S(2)}, u32[]{:S(2)}) collective-permute-start(s32[4,16]{1,0:T(4,128)S(1)} %broadcast_select_fusion.3), channel_id=1, source_target_pairs={{16,0},{24,8},{32,16},{40,24},{48,32},{56,40},{64,48},{72,56},{80,... | collective-permute-start | bytes 776 | tf_op jit(solution)/shard_map/ppermute | solution.py:10
  394.7 2.8 collective-permute-start.2
  397.5 27.6 %collective-permute-start.6 = (s32[4,16]{1,0:T(4,128)S(1)}, s32[4,16]{1,0:T(4,128)S(1)}, u32[]{:S(2)}, u32[]{:S(2)}) collective-permute-start(s32[4,16]{1,0:T(4,128)S(1)} %broadcast_select_fusion.5), channel_id=1, source_target_pairs={{248,0},{0,8},{8,16},{16,24},{24,32},{32,40},{40,48},{48,56},{56,6... | collective-permute-start | bytes 776 | tf_op jit(solution)/shard_map/ppermute | solution.py:10
  425.1 9.5 %collective-permute-start.8 = (s32[4,16]{1,0:T(4,128)S(1)}, s32[4,16]{1,0:T(4,128)S(1)}, u32[]{:S(2)}, u32[]{:S(2)}) collective-permute-start(s32[4,16]{1,0:T(4,128)S(1)} %collective-permute-done.6), channel_id=1, source_target_pairs={{248,0},{0,8},{8,16},{16,24},{24,32},{32,40},{40,48},{48,56},{56,6... | collective-permute-start | bytes 776 | tf_op jit(solution)/shard_map/ppermute | solution.py:10
  443.8 9.6 %copy-start.1 = (f32[4,2,128,128]{3,2,1,0:T(8,128)S(1)}, f32[4,2,128,128]{3,2,1,0:T(8,128)}, u32[]{:S(2)}) copy-start(f32[4,2,128,128]{3,2,1,0:T(8,128)} %param.3) | copy-start | bytes 1572868
  509.9 0.7 copy-start.4
Sparse Core Ops, SparseCore 0:
  9.1 58.6 all-gather.1
  510.0 111.2 all-reduce.2
where the time goes:
time: 639 us; the launch traced here: 631 us
  waiting for transfers between devices  477 us (75%)
  matrix products  75.1 us (12%)
  starting transfers between devices  34.4 us (5%)
  other arithmetic  15.6 us (2%)
  between operations  14.5 us (2%)
  local copies, waits for them, and re-layouts  13.7 us (2%)
    ppermute x10, waiting for transfers between devices, from_behind(): return lax.ppermute(block, axis, route)  308 us
    unnamed x3, waiting for transfers between devices  110 us
    all_gather x1, waiting for transfers between devices, on_device(): panel_vals = lax.all_gather(p_vals, 'col', axis=1, tiled=True)  59.3 us
    dot_general x3, matrix products, on_device(): jnp.einsum('isab,isobc->ioac', p_vals, mixed, precision=lax.Precision.HIG...  47.5 us
    ppermute x10, starting transfers between devices, from_behind(): return lax.ppermute(block, axis, route)  34.3 us
    dot_general x3, matrix products, on_device(): jnp.einsum('isolt,ltab->isoab', weights, panel_vals, precision=lax.Precis...  27.6 us
    select_n x3, other arithmetic, on_device(): panel_vals = jnp.where(taken, moved[0], panel_vals)  15.3 us
  transfers between devices with their start and end apart: 12, of which 11 were waited for; matrix products, arithmetic and copies ran while one was open for 6% of the time, Pallas kernels for 0%

commit v1 on v0

v1 whole, which is shorter than its diff:
```python
import jax
import jax.numpy as jnp
from jax import lax
from jax.experimental import pallas as pl
from jax.experimental.pallas import tpu as pltpu
from jax.sharding import PartitionSpec as P

MESH = pl.DeviceIdType.MESH
F32 = jnp.float32
BF16 = jnp.bfloat16
NX, NY, NZ = 4, 4, 8


def up(v, d, n):
    return lax.rem(v + (d + n), n)


def kernel(meta_ref, p_ref, out_ref, pt, tb, mbuf, sm, ag, bg, rot, stage, pvs, mt, aw, ct, r1, r2, fo, fi,
           tbs, tbr, ms, mr, ays, ayr, axs, axr, zs, zr, cs, cr, ys, yr, fs, fr, loc):
    row = lax.axis_index("row")
    col = lax.axis_index("col")
    z, yh, q = row // 4, lax.rem(row // 2, 2), lax.rem(row, 2)
    yl, x = col // 4, lax.rem(col, 4)
    y = 2 * yh + yl

    def dev(x_, y_, z_, q_):
        return (z_ * 4 + (y_ // 2) * 2 + q_, lax.rem(y_, 2) * 4 + x_)

    def rcopy(src, dst, s, r, to):
        return pltpu.make_async_remote_copy(
            src_ref=src, dst_ref=dst, send_sem=s, recv_sem=r, device_id=to, device_id_type=MESH
        )

    plane = [(dx, dy) for dy in range(NY) for dx in range(NX) if (dx, dy) != (0, 0)]
    metas = [(lev, dh, dq) for lev in range(4) for dh in range(2) for dq in range(2) if (lev, dh, dq) != (1, 0, 0)]

    def flip(v, d):
        return lax.rem(v + d, 2)

    def level_dev(dz, dh, dq):
        return dev(x, 2 * flip(yh, dh) + yl, up(z, dz, NZ), flip(q, dq))

    barrier = pltpu.get_barrier_semaphore()
    for dx, dy in plane:
        pl.semaphore_signal(barrier, inc=1, device_id=dev(up(x, -dx, NX), up(y, -dy, NY), z, q), device_id_type=MESH)
    for lev, dh, dq in metas:
        pl.semaphore_signal(barrier, inc=1, device_id=level_dev(lev - 1, dh, dq), device_id_type=MESH)

    lane = lax.broadcasted_iota(jnp.int32, (128, 128), 1) // 32
    for e in range(2):
        for l in range(4):
            pt[l, e] = p_ref[l, e].T
        for yy in range(NY):
            packed = None
            for l in range(4):
                t = pt[l, e]
                if l != yy:
                    t = pltpu.roll(t, (32 * (l - yy)) % 128, 1)
                packed = t if packed is None else jnp.where(lane == l, t, packed)
            for xx in range(NX):
                tb[yy, xx, e] = packed[32 * xx:32 * xx + 32].reshape(4, 8, 128)

    pl.semaphore_wait(barrier, len(plane) + len(metas))

    own = [pltpu.make_async_copy(tb.at[y, x], bg.at[q, 1, yh, pl.ds(2 * col, 2)], loc.at[0]),
           pltpu.make_async_copy(meta_ref, mbuf.at[q * 8 + 2 + yh], loc.at[1]),
           pltpu.make_async_copy(pt.at[:, :, pl.ds(32 * y, 32)], ag.at[x, y], loc.at[2])]
    for c in own:
        c.start()
    sends = []
    for n, (dx, dy) in enumerate(plane):
        xx, yy = up(x, dx, NX), up(y, dy, NY)
        c = rcopy(tb.at[yy, xx], bg.at[q, 1, yh, pl.ds(2 * col, 2)], tbs.at[n], tbr.at[n], dev(xx, yy, z, q))
        c.start()
        sends.append(c)
    msends = []
    for n, (lev, dh, dq) in enumerate(metas):
        c = rcopy(meta_ref, mbuf.at[q * 8 + lev * 2 + yh], ms.at[n], mr.at[n], level_dev(1 - lev, dh, dq))
        c.start()
        msends.append(c)
    asends = []
    for dy in range(1, NY):
        yy = up(y, dy, NY)
        c = rcopy(pt.at[:, :, pl.ds(32 * yy, 32)], ag.at[x, y], ays.at[dy], ayr.at[dy], dev(x, yy, z, q))
        c.start()
        asends.append(c)
    for c in own:
        c.wait()
    for c in sends:
        c.wait_recv()

    zdn, zup = up(z, -1, NZ), up(z, 1, NZ)
    lower, upper, mate = dev(x, y, zdn, q), dev(x, y, zup, q), dev(x, y, z, 1 - q)
    z2 = rcopy(bg.at[q, 1], bg.at[q, 2], zs.at[0], zr.at[0], lower)
    z0 = rcopy(bg.at[q, 1, 1], bg.at[q, 0, 1], zs.at[1], zr.at[1], upper)
    c1 = rcopy(bg.at[q, 1], bg.at[q, 1], cs.at[0], cr.at[0], mate)
    z2.start()
    z0.start()
    c1.start()

    for c in asends:
        c.wait_recv()
    xp, xm, xf = up(x, 1, NX), up(x, -1, NX), up(x, 2, NX)
    right, left = dev(xp, y, z, q), dev(xm, y, z, q)
    x0 = rcopy(ag.at[x], ag.at[x], axs.at[0], axr.at[0], right)
    x1 = rcopy(ag.at[x], ag.at[x], axs.at[1], axr.at[1], left)
    x0.start()
    x1.start()

    for c in msends:
        c.wait()
    mc = pltpu.make_async_copy(mbuf, sm, loc.at[3])
    mc.start()

    def expand(qs, lev, h):
        def step(s, carry):
            t = bg[qs, lev, h, s].reshape(32, 128)
            for k in range(4):
                u = t if k == 0 else pltpu.roll(t, 32 * k, 1)
                rot[k, qs * 8 + lev * 2 + h, s] = u.reshape(4, 8, 128)
            return carry
        lax.fori_loop(0, 16, step, 0)

    expand(q, 1, 0)
    expand(q, 1, 1)

    z2.wait_recv()
    z3a = rcopy(bg.at[q, 2, 0], bg.at[q, 3, 0], zs.at[2], zr.at[2], lower)
    z3b = rcopy(bg.at[q, 2, 1], bg.at[q, 3, 1], zs.at[3], zr.at[3], lower)
    z3a.start()

    @pl.when(q == 0)
    def _():
        z3b.start()

    c2 = rcopy(bg.at[q, 2], bg.at[q, 2], cs.at[1], cr.at[1], mate)
    c2.start()
    z0.wait_recv()
    c0 = rcopy(bg.at[1, 0, 1], bg.at[1, 0, 1], cs.at[4], cr.at[4], mate)

    @pl.when(q == 1)
    def _():
        c0.start()

    c1.wait_recv()
    expand(1 - q, 1, 0)
    expand(1 - q, 1, 1)

    x0.wait_recv()
    x1.wait_recv()
    x2 = rcopy(ag.at[xm, pl.ds(0, 2)], ag.at[xm, pl.ds(0, 2)], axs.at[2], axr.at[2], right)
    x3 = rcopy(ag.at[xp, pl.ds(2, 2)], ag.at[xp, pl.ds(2, 2)], axs.at[3], axr.at[3], left)
    x2.start()
    x3.start()

    expand(q, 2, 0)
    expand(q, 2, 1)
    expand(q, 0, 1)

    @pl.when(q == 0)
    def _():
        c0.wait_recv()
        expand(1, 0, 1)

    c2.wait_recv()
    expand(1 - q, 2, 0)
    expand(1 - q, 2, 1)
    z3a.wait_recv()
    c3a = rcopy(bg.at[q, 3, 0], bg.at[q, 3, 0], cs.at[2], cr.at[2], mate)
    c3b = rcopy(bg.at[0, 3, 1], bg.at[0, 3, 1], cs.at[3], cr.at[3], mate)
    c3a.start()
    expand(q, 3, 0)

    @pl.when(q == 0)
    def _():
        z3b.wait_recv()
        c3b.start()
        expand(0, 3, 1)

    c3a.wait_recv()
    expand(1 - q, 3, 0)

    @pl.when(q == 1)
    def _():
        c3b.wait_recv()
        expand(0, 3, 1)

    x2.wait_recv()
    x3.wait_recv()
    mc.wait()

    lane8 = lax.broadcasted_iota(jnp.int32, (8, 128), 1) // 32
    sel = [lane8 == j for j in range(3)]

    def spread(v):
        r = jnp.where(sel[2], v[2], v[3])
        r = jnp.where(sel[1], v[1], r)
        return jnp.where(sel[0], v[0], r)

    def product(h, l, s4):
        mine = q * 8 + 2 + h
        slot, kl, rt, win = [], [], [], []
        for j in range(4):
            s = 4 * s4 + j
            k = sm[mine, l, s]
            g = k // 4
            kk = lax.rem(k, 4)
            off = lax.rem(row // 4 * 4 + 2 * h + q + s // 2 - g + 64, 32)
            w = off < 3
            lev = jnp.where(w, lax.rem(g // 4 - z + 9, 8), 1)
            slot.append(lax.rem(g, 2) * 8 + lev * 2 + lax.rem(g // 2, 2))
            kl.append(kk)
            rt.append(lax.rem(j + 4 - kk, 4))
            win.append(w)
        for s2 in range(16):
            stage[s2] = spread([rot[rt[j], slot[j], s2] for j in range(4)])
            pvs[s2] = spread([jnp.where(win[j], sm[slot[j], kl[j], s2], -1) for j in range(4)])

        def some(oq, carry):
            oc = [sm[mine, l, 16 + oq * 4 + n] for n in range(4)]
            acc = [jnp.zeros((4, 8, 128), F32)] * 4
            for s2 in range(16):
                b = stage[s2]
                v = pvs[s2]
                for n in range(4):
                    acc[n] = acc[n] + jnp.where((v == oc[n])[None], b, 0.0)
            for n in range(4):
                a = acc[n].reshape(32, 128)
                hi = a.astype(BF16)
                lo = (a - hi.astype(F32)).astype(BF16)
                at = pl.ds(pl.multiple_of(oq * 128 + n * 32, 32), 32)
                mt[at, 0:128] = hi
                mt[at, 128:256] = lo
            return carry

        lax.fori_loop(0, 4, some, 0)
        a = ag[pl.ds(2 * (s4 % 2), 2), 2 * h + s4 // 2, l].reshape(128, 128)
        hi = a.astype(BF16)
        aw[0:128, 0:128] = hi
        aw[0:128, 128:256] = (a - hi.astype(F32)).astype(BF16)
        aw[128:256, 0:128] = hi
        r = jnp.dot(mt[...], aw[...], preferred_element_type=F32)
        r = r[:, :128] + r[:, 128:]
        for half in range(2):
            part = r[256 * half:256 * half + 256]
            if s4 == 0:
                ct[h, half, l] = part
            else:
                ct[h, half, l] = ct[h, half, l] + part

    aw[128:256, 128:256] = jnp.zeros((128, 128), BF16)
    for s4 in range(4):
        def step(i, carry, s4=s4):
            product(i // 4, lax.rem(i, 4), s4)
            return carry
        lax.fori_loop(0, 8, step, 0)

    yp, ym, yf = up(y, 1, NY), up(y, -1, NY), up(y, 2, NY)
    above, below = dev(x, yp, z, q), dev(x, ym, z, q)

    def piece(y_):
        return ct.at[y_ // 2, lax.rem(y_, 2)]

    s1a = rcopy(piece(yf).at[pl.ds(0, 2)], r1.at[0], ys.at[0], yr.at[0], above)
    s1b = rcopy(piece(yf).at[pl.ds(2, 2)], r1.at[1], ys.at[1], yr.at[1], below)
    s1a.start()
    s1b.start()
    s1a.wait_recv()
    a = piece(yp).at[pl.ds(0, 2)]
    a[...] = a[...] + r1[0]
    s2a = rcopy(piece(yp), r2.at[0], ys.at[2], yr.at[2], above)
    s2a.start()
    s1b.wait_recv()
    b = piece(ym).at[pl.ds(2, 2)]
    b[...] = b[...] + r1[1]
    s2b = rcopy(piece(ym), r2.at[1], ys.at[3], yr.at[3], below)
    s2b.start()
    s2a.wait_recv()
    s2b.wait_recv()
    mine = piece(y)
    for l in range(4):
        t = mine[l] + r2[0, l] + r2[1, l]
        for xx in range(NX):
            fo[xx, l] = t[64 * xx:64 * xx + 64]

    fsends = []
    for dx in range(1, NX):
        xx = up(x, dx, NX)
        c = rcopy(fo.at[xx], fi.at[x], fs.at[dx], fr.at[dx], dev(xx, y, z, q))
        c.start()
        fsends.append(c)
    lf = pltpu.make_async_copy(fo.at[x], fi.at[x], loc.at[4])
    lf.start()
    lf.wait()
    for c in fsends:
        c.wait_recv()
    for l in range(4):
        for e in range(2):
            t = jnp.concatenate([fi[xx, l, 32 * e:32 * e + 32] for xx in range(NX)], axis=0)
            out_ref[l, e] = t.T

    for c in sends + asends + fsends + [z2, z0, c1, c2, z3a, c3a, x0, x1, x2, x3, s1a, s1b, s2a, s2b]:
        c.wait_send()

    @pl.when(q == 0)
    def _():
        z3b.wait_send()
        c3b.wait_send()

    @pl.when(q == 1)
    def _():
        c0.wait_send()


def on_device(p_vals, p_cols, out_cols):
    meta = jnp.pad(jnp.concatenate([p_cols, out_cols], axis=1), ((0, 4), (0, 96)))
    dma = pltpu.SemaphoreType.DMA
    vm = pltpu.VMEM
    return pl.pallas_call(
        kernel,
        out_shape=jax.ShapeDtypeStruct((4, 2, 128, 128), F32),
        in_specs=[pl.BlockSpec(memory_space=pltpu.VMEM)] * 2,
        out_specs=pl.BlockSpec(memory_space=pltpu.VMEM),
        scratch_shapes=[
            vm((4, 2, 128, 128), F32),
            vm((4, 4, 2, 4, 8, 128), F32),
            vm((16, 8, 128), jnp.int32),
            pltpu.SMEM((16, 8, 128), jnp.int32),
            vm((4, 4, 4, 2, 32, 128), F32),
            vm((2, 4, 2, 16, 4, 8, 128), F32),
            vm((4, 16, 16, 4, 8, 128), F32),
            vm((16, 4, 8, 128), F32),
            vm((16, 8, 128), jnp.int32),
            vm((512, 256), BF16),
            vm((256, 256), BF16),
            vm((2, 2, 4, 256, 128), F32),
            vm((2, 2, 256, 128), F32),
            vm((2, 4, 256, 128), F32),
            vm((4, 4, 64, 128), F32),
            vm((4, 4, 64, 128), F32),
            dma((15,)), dma((15,)), dma((15,)), dma((15,)), dma((4,)), dma((4,)), dma((4,)), dma((4,)),
            dma((4,)), dma((4,)), dma((5,)), dma((5,)), dma((4,)), dma((4,)), dma((4,)), dma((4,)), dma((5,)),
        ],
        compiler_params=pltpu.CompilerParams(collective_id=0, has_side_effects=True),
        name="square",
    )(meta, p_vals)


def solution(mesh):
    placed = (P("row", "col", None, None), P("row", None), P("row", None))
    return jax.shard_map(
        on_device,
        mesh=mesh,
        in_specs=placed,
        out_specs=P("row", "col", None, None),
        check_vma=False,
    )
```

time: 639 us -> 115 us (0.18); the launches traced: 631 us -> 114 us
  waiting for transfers between devices: 477 us -> 0 us
  Pallas kernels: 0 us -> 110 us
  matrix products: 75.1 us -> 0 us
  starting transfers between devices: 34.4 us -> 0 us
  other arithmetic: 15.6 us -> 0.77 us
  between operations: 14.5 us -> 0.01 us
  local copies, waits for them, and re-layouts: 13.7 us -> 2.47 us
    ppermute x10 -> x0, waiting for transfers between devices: 308 us -> none  [from_behind(): return lax.ppermute(block, axis, route)]
    pallas_call x0 -> x1, Pallas kernels: none -> 110 us  [on_device(): pl.pallas_call(kernel, out_shape=jax.ShapeDtypeStruct((4, 2, 128, 128), F...]
    unnamed x3 -> x0, waiting for transfers between devices: 110 us -> none
    dot_general x6 -> x0, matrix products: 75.1 us -> none  [the longest x3 47.5 us: on_device(): jnp.einsum('isab,isobc->ioac', p_vals, mixed, precision=lax.Precision.HIG...]
    all_gather x1 -> x0, waiting for transfers between devices: 59.3 us -> none  [on_device(): panel_vals = lax.all_gather(p_vals, 'col', axis=1, tiled=True)]
    ppermute x10 -> x0, starting transfers between devices: 34.3 us -> none  [from_behind(): return lax.ppermute(block, axis, route)]
    select_n x6 -> x0, other arithmetic: 15.3 us -> none  [the longest x3 15.3 us: on_device(): panel_vals = jnp.where(taken, moved[0], panel_vals)]
    all_gather x1 -> x0, local copies, waits for them, and re-layouts: 6.59 us -> none  [on_device(): panel_vals = lax.all_gather(p_vals, 'col', axis=1, tiled=True)]
  transfers between devices with their start and end apart: 12 -> 0, of which waited for: 11 -> 0; matrix products, arithmetic and copies ran while one was open for 6% -> 0% of each run, Pallas kernels for 0% -> 0%
where the time goes in v1:
time: 115 us; the launch traced here: 114 us
  Pallas kernels  110 us (96%)
  local copies, waits for them, and re-layouts  2.47 us (2%)
    pallas_call x1, Pallas kernels, on_device(): pl.pallas_call(kernel, out_shape=jax.ShapeDtypeStruct((4, 2, 128, 128), F...  110 us

profile of v1, /device:TPU:1, one launch (start us, length us, event | category | flops | bytes accessed | tf_op | source)
XLA Modules:
  0.0 113.8 jit_solution(8452709267502473681)
XLA Ops:
  0.0 0.8 pad_add_fusion
  0.8 0.6 pad.4.meta_ref
  1.4 110.5 %square.1 = f32[4,2,128,128]{3,2,1,0:T(8,128)} custom-call(s32[8,128]{1,0:T(8,128)} %pad.4.meta_ref, f32[4,2,128,128]{3,2,1,0:T(8,128)} %p_ref.1), custom_call_target="tpu_custom_call" | custom-call | tf_op jit(solution)/shard_map/square/pallas_call | solution.py:319
  111.9 1.9 %copy.5 = f32[4,2,128,128]{3,2,1,0:T(8,128)} copy(f32[4,2,128,128]{3,2,1,0:T(8,128)} %square.1) | data formatting | bytes 1048576

commit v2 on v1

--- a/solution.py
+++ b/solution.py
@@ -15,7 +15,7 @@
     return lax.rem(v + (d + n), n)
 
 
-def kernel(meta_ref, p_ref, out_ref, pt, tb, mbuf, sm, ag, bg, rot, stage, pvs, mt, aw, ct, r1, r2, fo, fi,
+def kernel(meta_ref, p_ref, out_ref, pt, tb, mbuf, sm, ix, ixs, ag, bg, rot, pvs, mt, aw, ct, r1, r2, fo, fi,
            tbs, tbr, ms, mr, ays, ayr, axs, axr, zs, zr, cs, cr, ys, yr, fs, fr, loc):
     row = lax.axis_index("row")
     col = lax.axis_index("col")
@@ -112,14 +112,60 @@
     mc = pltpu.make_async_copy(mbuf, sm, loc.at[3])
     mc.start()
 
+    mc.wait()
+    lane8 = lax.broadcasted_iota(jnp.int32, (8, 128), 1) // 32
+    sel = [lane8 == j for j in range(3)]
+
+    def spread(v):
+        r = jnp.where(sel[2], v[2], v[3])
+        r = jnp.where(sel[1], v[1], r)
+        return jnp.where(sel[0], v[0], r)
+
     def expand(qs, lev, h):
-        def step(s, carry):
-            t = bg[qs, lev, h, s].reshape(32, 128)
-            for k in range(4):
-                u = t if k == 0 else pltpu.roll(t, 32 * k, 1)
-                rot[k, qs * 8 + lev * 2 + h, s] = u.reshape(4, 8, 128)
+        slot = qs * 8 + lev * 2 + h
+        for s in range(16):
+            pvs[s] = spread([sm[slot, l, s] for l in range(4)])
+
+        def step(i, carry):
+            acc = [jnp.zeros((4, 8, 128), F32)] * 2
+            v = [pvs[2 * i + e] for e in range(2)]
+            for s in range(16):
+                b = bg[qs, lev, h, s]
+                w = pvs[s]
+                for e in range(2):
+                    acc[e] = acc[e] + jnp.where((w == v[e])[None], b, 0.0)
+            for e in range(2):
+                t = acc[e].reshape(32, 128)
+                for k in range(4):
+                    u = t if k == 0 else pltpu.roll(t, 32 * k, 1)
+                    rot[(k * 16 + slot) * 16 + 2 * i + e] = u.reshape(4, 8, 128)
             return carry
-        lax.fori_loop(0, 16, step, 0)
+        lax.fori_loop(0, 8, step, 0)
+
+    rot[1024] = jnp.zeros((4, 8, 128), F32)
+
+    def pick(i, carry):
+        h, l, s4 = i // 16, lax.rem(i // 4, 4), lax.rem(i, 4)
+        mine = q * 8 + 2 + h
+        outs = mbuf[mine, pl.ds(l, 1)]
+        for j in range(4):
+            s = 4 * s4 + j
+            k = sm[mine, l, s]
+            g = k // 4
+            kk = lax.rem(k, 4)
+            w = lax.rem(row // 4 * 4 + 2 * h + q + s // 2 - g + 64, 32) < 3
+            lev = jnp.where(w, lax.rem(g // 4 - z + 9, 8), 1)
+            slot = lax.rem(g, 2) * 8 + lev * 2 + lax.rem(g // 2, 2)
+            base = (lax.rem(j + 4 - kk, 4) * 16 + slot) * 16
+            v = jnp.full((1, 128), 1024, jnp.int32)
+            for s2 in reversed(range(16)):
+                v = jnp.where(outs == jnp.where(w, sm[slot, kk, s2], -1), base + s2, v)
+            ix[pl.ds(i * 4 + j, 1)] = v
+        return carry
+
+    lax.fori_loop(0, 32, pick, 0)
+    ic = pltpu.make_async_copy(ix, ixs, loc.at[3])
+    ic.start()
 
     expand(q, 1, 0)
     expand(q, 1, 1)
@@ -165,81 +211,18 @@
     c2.wait_recv()
     expand(1 - q, 2, 0)
     expand(1 - q, 2, 1)
-    z3a.wait_recv()
-    c3a = rcopy(bg.at[q, 3, 0], bg.at[q, 3, 0], cs.at[2], cr.at[2], mate)
-    c3b = rcopy(bg.at[0, 3, 1], bg.at[0, 3, 1], cs.at[3], cr.at[3], mate)
-    c3a.start()
-    expand(q, 3, 0)
-
-    @pl.when(q == 0)
-    def _():
-        z3b.wait_recv()
-        c3b.start()
-        expand(0, 3, 1)
-
-    c3a.wait_recv()
-    expand(1 - q, 3, 0)
-
-    @pl.when(q == 1)
-    def _():
-        c3b.wait_recv()
-        expand(0, 3, 1)
-
-    x2.wait_recv()
-    x3.wait_recv()
-    mc.wait()
-
-    lane8 = lax.broadcasted_iota(jnp.int32, (8, 128), 1) // 32
-    sel = [lane8 == j for j in range(3)]
-
-    def spread(v):
-        r = jnp.where(sel[2], v[2], v[3])
-        r = jnp.where(sel[1], v[1], r)
-        return jnp.where(sel[0], v[0], r)
-
-    def product(h, l, s4):
-        mine = q * 8 + 2 + h
-        slot, kl, rt, win = [], [], [], []
-        for j in range(4):
-            s = 4 * s4 + j
-            k = sm[mine, l, s]
-            g = k // 4
-            kk = lax.rem(k, 4)
-            off = lax.rem(row // 4 * 4 + 2 * h + q + s // 2 - g + 64, 32)
-            w = off < 3
-            lev = jnp.where(w, lax.rem(g // 4 - z + 9, 8), 1)
-            slot.append(lax.rem(g, 2) * 8 + lev * 2 + lax.rem(g // 2, 2))
-            kl.append(kk)
-            rt.append(lax.rem(j + 4 - kk, 4))
-            win.append(w)
-        for s2 in range(16):
-            stage[s2] = spread([rot[rt[j], slot[j], s2] for j in range(4)])
-            pvs[s2] = spread([jnp.where(win[j], sm[slot[j], kl[j], s2], -1) for j in range(4)])
-
-        def some(oq, carry):
-            oc = [sm[mine, l, 16 + oq * 4 + n] for n in range(4)]
-            acc = [jnp.zeros((4, 8, 128), F32)] * 4
-            for s2 in range(16):
-                b = stage[s2]
-                v = pvs[s2]
-                for n in range(4):
-                    acc[n] = acc[n] + jnp.where((v == oc[n])[None], b, 0.0)
-            for n in range(4):
-                a = acc[n].reshape(32, 128)
-                hi = a.astype(BF16)
-                lo = (a - hi.astype(F32)).astype(BF16)
-                at = pl.ds(pl.multiple_of(oq * 128 + n * 32, 32), 32)
-                mt[at, 0:128] = hi
-                mt[at, 128:256] = lo
-            return carry
-
-        lax.fori_loop(0, 4, some, 0)
+    def product(h, l, s4, m):
+        for o in range(16):
+            a = spread([rot[ixs[(h * 4 + l) * 16 + 4 * s4 + j, 16 + o]] for j in range(4)]).reshape(32, 128)
+            hi = a.astype(BF16)
+            mt[m, 32 * o:32 * o + 32, 0:128] = hi
+            mt[m, 32 * o:32 * o + 32, 128:256] = (a - hi.astype(F32)).astype(BF16)
         a = ag[pl.ds(2 * (s4 % 2), 2), 2 * h + s4 // 2, l].reshape(128, 128)
         hi = a.astype(BF16)
-        aw[0:128, 0:128] = hi
-        aw[0:128, 128:256] = (a - hi.astype(F32)).astype(BF16)
-        aw[128:256, 0:128] = hi
-        r = jnp.dot(mt[...], aw[...], preferred_element_type=F32)
+        aw[m, 0:128, 0:128] = hi
+        aw[m, 0:128, 128:256] = (a - hi.astype(F32)).astype(BF16)
+        aw[m, 128:256, 0:128] = hi
+        r = jnp.dot(mt[m], aw[m], preferred_element_type=F32)
         r = r[:, :128] + r[:, 128:]
         for half in range(2):
             part = r[256 * half:256 * half + 256]
@@ -248,12 +231,45 @@
             else:
                 ct[h, half, l] = ct[h, half, l] + part
 
-    aw[128:256, 128:256] = jnp.zeros((128, 128), BF16)
-    for s4 in range(4):
-        def step(i, carry, s4=s4):
-            product(i // 4, lax.rem(i, 4), s4)
+    for m in range(2):
+        aw[m, 128:256, 128:256] = jnp.zeros((128, 128), BF16)
+
+    def products(h, s4):
+        def step(i, carry):
+            for m in range(2):
+                product(h, 2 * i + m, s4, m)
             return carry
-        lax.fori_loop(0, 8, step, 0)
+        lax.fori_loop(0, 2, step, 0)
+
+    x2.wait_recv()
+    x3.wait_recv()
+    ic.wait()
+    for s4 in range(2):
+        products(1 - yh, s4)
+        products(yh, s4)
+
+    z3a.wait_recv()
+    c3a = rcopy(bg.at[q, 3, 0], bg.at[q, 3, 0], cs.at[2], cr.at[2], mate)
+    c3b = rcopy(bg.at[0, 3, 1], bg.at[0, 3, 1], cs.at[3], cr.at[3], mate)
+    c3a.start()
+    expand(q, 3, 0)
+
+    @pl.when(q == 0)
+    def _():
+        z3b.wait_recv()
+        c3b.start()
+        expand(0, 3, 1)
+
+    c3a.wait_recv()
+    expand(1 - q, 3, 0)
+
+    @pl.when(q == 1)
+    def _():
+        c3b.wait_recv()
+        expand(0, 3, 1)
+
+    products(1 - yh, 2)
+    products(1 - yh, 3)
 
     yp, ym, yf = up(y, 1, NY), up(y, -1, NY), up(y, 2, NY)
     above, below = dev(x, yp, z, q), dev(x, ym, z, q)
@@ -265,6 +281,8 @@
     s1b = rcopy(piece(yf).at[pl.ds(2, 2)], r1.at[1], ys.at[1], yr.at[1], below)
     s1a.start()
     s1b.start()
+    products(yh, 2)
+    products(yh, 3)
     s1a.wait_recv()
     a = piece(yp).at[pl.ds(0, 2)]
     a[...] = a[...] + r1[0]
@@ -326,13 +344,14 @@
             vm((4, 4, 2, 4, 8, 128), F32),
             vm((16, 8, 128), jnp.int32),
             pltpu.SMEM((16, 8, 128), jnp.int32),
+            vm((128, 128), jnp.int32),
+            pltpu.SMEM((128, 128), jnp.int32),
             vm((4, 4, 4, 2, 32, 128), F32),
             vm((2, 4, 2, 16, 4, 8, 128), F32),
-            vm((4, 16, 16, 4, 8, 128), F32),
-            vm((16, 4, 8, 128), F32),
+            vm((1025, 4, 8, 128), F32),
             vm((16, 8, 128), jnp.int32),
-            vm((512, 256), BF16),
-            vm((256, 256), BF16),
+            vm((2, 512, 256), BF16),
+            vm((2, 256, 256), BF16),
             vm((2, 2, 4, 256, 128), F32),
             vm((2, 2, 256, 128), F32),
             vm((2, 4, 256, 128), F32),

time: 115 us -> 89.3 us (0.78)
  Pallas kernels: 110 us -> 84.6 us
    pallas_call x1, Pallas kernels: 110 us -> 84.6 us  [on_device(): pl.pallas_call(kernel, out_shape=jax.ShapeDtypeStruct((4, 2, 128, 128), F...]
where the time goes in v2:
time: 89.3 us; the launch traced here: 87.8 us
  Pallas kernels  84.6 us (95%)
  local copies, waits for them, and re-layouts  2.47 us (3%)
    pallas_call x1, Pallas kernels, on_device(): pl.pallas_call(kernel, out_shape=jax.ShapeDtypeStruct((4, 2, 128, 128), F...  84.6 us
    unnamed x1, local copies, waits for them, and re-layouts  1.87 us

profile of v2, /device:TPU:1, one launch (start us, length us, event | category | flops | bytes accessed | tf_op | source)
XLA Modules:
  0.0 87.8 jit_solution(11633969561284860115)
XLA Ops:
  0.0 0.8 pad_add_fusion
  0.8 0.6 pad.4.meta_ref
  1.4 84.6 %square.1 = f32[4,2,128,128]{3,2,1,0:T(8,128)} custom-call(s32[8,128]{1,0:T(8,128)} %pad.4.meta_ref, f32[4,2,128,128]{3,2,1,0:T(8,128)} %p_ref.1), custom_call_target="tpu_custom_call" | custom-call | tf_op jit(solution)/shard_map/square/pallas_call | solution.py:337
  86.0 1.9 %copy.5 = f32[4,2,128,128]{3,2,1,0:T(8,128)} copy(f32[4,2,128,128]{3,2,1,0:T(8,128)} %square.1) | data formatting | bytes 1048576

commit v3 on v0

v3 whole, which is shorter than its diff:
```python
import jax
import jax.numpy as jnp
from jax import lax
from jax.experimental import pallas as pl
from jax.experimental.pallas import tpu as pltpu
from jax.sharding import PartitionSpec as P

MESH = pl.DeviceIdType.MESH
F32 = jnp.float32
BF16 = jnp.bfloat16
NX, NY, NZ = 4, 4, 8


def up(v, d, n):
    return lax.rem(v + (d + n), n)


def kernel(p_ref, pc_ref, oc_ref, out_ref, pt, tb, mown, mbuf, sm, ix, ixs, ag, bg, rot, pvs, mt, aw, ct, r1, r2, fo, fi,
           tbs, tbr, ms, mr, ays, ayr, axs, axr, afs, afr, zs, zr, cs, cr, us, ur, vs, vr, fs, fr, loc):
    row = lax.axis_index("row")
    col = lax.axis_index("col")
    z, yh, q = lax.div(row, 4), lax.rem(lax.div(row, 2), 2), lax.rem(row, 2)
    yl, x = lax.div(col, 4), lax.rem(col, 4)
    y = 2 * yh + yl

    def dev(x_, y_, z_, q_):
        return (z_ * 4 + lax.div(y_, 2) * 2 + q_, lax.rem(y_, 2) * 4 + x_)

    def rcopy(src, dst, s, r, to):
        return pltpu.make_async_remote_copy(
            src_ref=src, dst_ref=dst, send_sem=s, recv_sem=r, device_id=to, device_id_type=MESH
        )

    started = []

    def go(c):
        c.start()
        started.append(c)
        return c

    plane = [(dx, dy) for dy in range(NY) for dx in range(NX) if (dx, dy) != (0, 0)]
    lower, upper, mate = dev(x, y, up(z, -1, NZ), q), dev(x, y, up(z, 1, NZ), q), dev(x, y, z, 1 - q)
    xp, xm = up(x, 1, NX), up(x, -1, NX)
    right, left = dev(xp, y, z, q), dev(xm, y, z, q)
    yp, ym, yf = up(y, 1, NY), up(y, -1, NY), up(y, 2, NY)
    above, below = dev(x, yp, z, q), dev(x, ym, z, q)

    barrier = pltpu.get_barrier_semaphore()
    for to in [dev(up(x, -dx, NX), up(y, -dy, NY), z, q) for dx, dy in plane] + [lower, upper, mate]:
        pl.semaphore_signal(barrier, inc=1, device_id=to, device_id_type=MESH)

    mown[...] = jnp.zeros((8, 128), jnp.int32)
    mown[0:4, 0:16] = pc_ref[...]
    mown[4:8, 0:16] = oc_ref[...]
    lane = lax.div(lax.broadcasted_iota(jnp.int32, (128, 128), 1), 32)
    for e in range(2):
        for l in range(4):
            pt[l, e] = p_ref[l, e].T
        for yy in range(NY):
            packed = None
            for l in range(4):
                t = pt[l, e]
                if l != yy:
                    t = pltpu.roll(t, (32 * (l - yy)) % 128, 1)
                packed = t if packed is None else jnp.where(lane == l, t, packed)
            for xx in range(NX):
                tb[e, yy, xx] = packed[32 * xx:32 * xx + 32].reshape(4, 8, 128)
    rot[1024] = jnp.zeros((4, 8, 128), F32)
    for m in range(2):
        aw[m, 128:256, 128:256] = jnp.zeros((128, 128), BF16)

    pl.semaphore_wait(barrier, len(plane) + 3)

    my = go(rcopy(mown, mbuf.at[q * 8 + 2 + yh], ms.at[0], mr.at[0], dev(x, yf, z, q)))
    own = [pltpu.make_async_copy(mown, mbuf.at[q * 8 + 2 + yh], loc.at[0])]
    own += [pltpu.make_async_copy(tb.at[e, y, x], bg.at[q, 1, yh, e, col], loc.at[1 + e]) for e in range(2)]
    own += [pltpu.make_async_copy(pt.at[:, :, pl.ds(32 * y, 32)], ag.at[x, y], loc.at[3])]
    for c in own:
        c.start()

    def pieces(e):
        out = []
        for n, (dx, dy) in enumerate(plane):
            xx, yy = up(x, dx, NX), up(y, dy, NY)
            out.append(go(rcopy(tb.at[e, yy, xx], bg.at[q, 1, yh, e, col], tbs.at[e, n], tbr.at[e, n], dev(xx, yy, z, q))))
        return out

    b0 = pieces(0)
    rows_y = pt.at[:, :, pl.ds(32 * y, 32)]

    def beside(src, ys):
        return [rcopy(src, ag.at[x, ys], axs.at[n, ys], axr.at[n, ys], (right, left)[n]) for n in range(2)]

    for c in beside(rows_y, y):
        c.start()
    for dy in (1, 3, 2):
        if dy == 2:
            b1 = pieces(1)
        yy = up(y, dy, NY)
        go(rcopy(pt.at[:, :, pl.ds(32 * yy, 32)], ag.at[x, y], ays.at[dy], ayr.at[y], dev(x, yy, z, q)))

    for c in own:
        c.wait()
    my.wait_recv()
    m2 = go(rcopy(mbuf.at[pl.ds(q * 8 + 2, 2)], mbuf.at[pl.ds(q * 8 + 4, 2)], ms.at[1], mr.at[1], lower))
    m0 = go(rcopy(mbuf.at[q * 8 + 3], mbuf.at[q * 8 + 1], ms.at[2], mr.at[2], upper))
    m2.wait_recv()
    m3 = go(rcopy(mbuf.at[pl.ds(q * 8 + 4, 2)], mbuf.at[pl.ds(q * 8 + 6, 2)], ms.at[3], mr.at[3], lower))

    def level1(e):
        a = go(rcopy(bg.at[q, 1, :, e], bg.at[q, 2, :, e], zs.at[0, e], zr.at[0, e], lower))
        b = go(rcopy(bg.at[q, 1, 1, e], bg.at[q, 0, 1, e], zs.at[1, e], zr.at[1, e], upper))
        return a, b

    for c in b0:
        c.wait_recv()
    za0, zb0 = level1(0)
    m0.wait_recv()
    m3.wait_recv()
    mm = go(rcopy(mbuf.at[pl.ds(q * 8 + 1, 7)], mbuf.at[pl.ds(q * 8 + 1, 7)], ms.at[4], mr.at[4], mate))
    mm.wait_recv()
    mc = pltpu.make_async_copy(mbuf, sm, loc.at[0])
    mc.start()
    mc.wait()

    def pick(i, carry):
        h, l, s4 = lax.div(i, 16), lax.rem(lax.div(i, 4), 4), lax.rem(i, 4)
        mine = q * 8 + 2 + h
        outs = mbuf[mine, pl.ds(4 + l, 1)]
        for j in range(4):
            s = 4 * s4 + j
            k = sm[mine, l, s]
            g = lax.div(k, 4)
            kk = lax.rem(k, 4)
            w = lax.rem(4 * z + 2 * h + q + lax.div(s, 2) - g + 64, 32) < 3
            lev = jnp.where(w, lax.rem(lax.div(g, 4) - z + 9, 8), 1)
            slot = lax.rem(g, 2) * 8 + lev * 2 + lax.rem(lax.div(g, 2), 2)
            base = (lax.rem(j + 4 - kk, 4) * 16 + slot) * 16
            v = jnp.full((1, 128), 1024, jnp.int32)
            for p in range(16):
                v = jnp.where(outs == sm[slot, kk, 2 * (p % 8) + p // 8], base + p, v)
            ix[pl.ds(i * 4 + j, 1)] = jnp.where(w, v, 1024)
        return carry

    lax.fori_loop(0, 32, pick, 0)
    ic = pltpu.make_async_copy(ix, ixs, loc.at[0])
    ic.start()

    for c in b1:
        c.wait_recv()
    za1, zb1 = level1(1)
    c1 = go(rcopy(bg.at[q, 1], bg.at[q, 1], cs.at[0], cr.at[0], mate))

    direct = [beside(ag.at[x, ys], ys) for ys in range(NY)]
    for ys in range(NY):
        @pl.when(y != ys)
        def _(ys=ys):
            rcopy(rows_y, ag.at[x, ys], ays.at[0], ayr.at[ys], right).wait_recv()
            for c in direct[ys]:
                c.start()

    def onward(ys):
        n = ys % 2
        direct[ys][n].wait_recv()
        ref = ag.at[(xm, xp)[n], ys]
        return go(rcopy(ref, ref, afs.at[ys], afr.at[ys], (right, left)[n]))

    lane8 = lax.div(lax.broadcasted_iota(jnp.int32, (8, 128), 1), 32)
    sel = [lane8 == j for j in range(3)]

    def spread(v):
        r = jnp.where(sel[2], v[2], v[3])
        r = jnp.where(sel[1], v[1], r)
        return jnp.where(sel[0], v[0], r)

    def expand(qs, lev, h):
        slot = qs * 8 + lev * 2 + h
        for p in range(16):
            pvs[p] = spread([sm[slot, l, 2 * (p % 8) + p // 8] for l in range(4)])

        def step(i, carry):
            acc = [jnp.zeros((4, 8, 128), F32)] * 2
            v = [pvs[2 * i + n] for n in range(2)]
            for p in range(16):
                b = bg[qs, lev, h, p // 8, p % 8]
                w = pvs[p]
                for n in range(2):
                    acc[n] = acc[n] + jnp.where((w == v[n])[None], b, 0.0)
            for n in range(2):
                t = acc[n].reshape(32, 128)
                for k in range(4):
                    u = t if k == 0 else pltpu.roll(t, 32 * k, 1)
                    rot[(k * 16 + slot) * 16 + 2 * i + n] = u.reshape(4, 8, 128)
            return carry
        lax.fori_loop(0, 8, step, 0)

    def both(qs, lev):
        def step(h, carry):
            expand(qs, lev, h)
            return carry
        lax.fori_loop(0, 2, step, 0)

    def level2(e, za):
        za.wait_recv()
        a = go(rcopy(bg.at[q, 2, 0, e], bg.at[q, 3, 0, e], zs.at[2, e], zr.at[2, e], lower))
        return a

    zc0 = level2(0, za0)
    both(q, 1)
    c1.wait_recv()
    both(1 - q, 1)

    far = [onward(0), onward(1)]
    zc1 = level2(1, za1)
    zd = [rcopy(bg.at[0, 2, 1, e], bg.at[0, 3, 1, e], zs.at[3, e], zr.at[3, e], lower) for e in range(2)]

    @pl.when(q == 0)
    def _():
        for c in zd:
            c.start()

    c2 = go(rcopy(bg.at[q, 2], bg.at[q, 2], cs.at[1], cr.at[1], mate))
    zb0.wait_recv()
    zb1.wait_recv()
    c0 = rcopy(bg.at[1, 0, 1], bg.at[1, 0, 1], cs.at[4], cr.at[4], mate)

    @pl.when(q == 1)
    def _():
        c0.start()

    both(q, 2)
    far += [onward(2), onward(3)]
    c2.wait_recv()
    both(1 - q, 2)

    @pl.when(q == 0)
    def _():
        c0.wait_recv()

    expand(1, 0, 1)

    @pl.when(q == 0)
    def _():
        expand(0, 0, 1)

    def product(h, l, s4, m, first):
        for o in range(16):
            a = spread([rot[ixs[(h * 4 + l) * 16 + 4 * s4 + j, o]] for j in range(4)]).reshape(32, 128)
            hi = a.astype(BF16)
            mt[m, 32 * o:32 * o + 32, 0:128] = hi
            mt[m, 32 * o:32 * o + 32, 128:256] = (a - hi.astype(F32)).astype(BF16)
        a = ag[pl.ds(2 * lax.rem(s4, 2), 2), 2 * h + lax.div(s4, 2), l].reshape(128, 128)
        hi = a.astype(BF16)
        aw[m, 0:128, 0:128] = hi
        aw[m, 0:128, 128:256] = (a - hi.astype(F32)).astype(BF16)
        aw[m, 128:256, 0:128] = hi
        r = jnp.dot(mt[m], aw[m], preferred_element_type=F32)
        r = r[:, :128] + r[:, 128:]
        for half in range(2):
            part = r[256 * half:256 * half + 256]
            ct[h, half, l] = part if first else ct[h, half, l] + part

    def early(h):
        for ys in (2 * h, 2 * h + 1):
            direct[ys][1 - ys % 2].wait_recv()
            far[ys].wait_recv()
        for s4 in range(2):
            def step(i, carry, s4=s4):
                for m in range(2):
                    product(h, 2 * i + m, s4, m, s4 == 0)
                return carry
            lax.fori_loop(0, 2, step, 0)

    ic.wait()
    early(0)
    zc0.wait_recv()
    zc1.wait_recv()
    c3a = go(rcopy(bg.at[q, 3, 0], bg.at[q, 3, 0], cs.at[2], cr.at[2], mate))
    c3b = rcopy(bg.at[0, 3, 1], bg.at[0, 3, 1], cs.at[3], cr.at[3], mate)
    expand(q, 3, 0)
    early(1)

    @pl.when(q == 0)
    def _():
        for c in zd:
            c.wait_recv()
        c3b.start()

    c3a.wait_recv()
    expand(1 - q, 3, 0)

    @pl.when(q == 1)
    def _():
        c3b.wait_recv()
        expand(0, 3, 1)

    def piece(y_, lp, part):
        return ct.at[lax.div(y_, 2), lax.rem(y_, 2), pl.ds(2 * lp, 2), pl.ds(128 * part, 128)]

    def rest(h, lp):
        def step(i, carry):
            for m in range(2):
                product(h, 2 * lp + m, 2 + i, m, False)
            return carry
        lax.fori_loop(0, 2, step, 0)

    def hop1(d, lp):
        return go(rcopy(piece(yf, lp, d), r1.at[d, lp], us.at[d, lp], ur.at[d, lp], (above, below)[d]))

    def hop2(d, part, lp):
        return go(rcopy(piece((yp, ym)[d], lp, part), r2.at[d, pl.ds(2 * lp, 2), pl.ds(128 * part, 128)],
                        vs.at[d, part, lp], vr.at[d, part, lp], (above, below)[d]))

    u, v = {}, {}
    for lp in range(2):
        rest(1 - yh, lp)
        for d in range(2):
            u[d, lp] = hop1(d, lp)
    for lp in range(2):
        rest(yh, lp)
        for d in range(2):
            v[d, 1 - d, lp] = hop2(d, 1 - d, lp)
    for lp in range(2):
        for d in range(2):
            u[d, lp].wait_recv()
            a = piece((yp, ym)[d], lp, d)
            a[...] = a[...] + r1[d, lp]
            v[d, d, lp] = hop2(d, d, lp)

    fsend = {}
    for lp in range(2):
        for d in range(2):
            for part in range(2):
                v[d, part, lp].wait_recv()
        for k in range(2):
            l = 2 * lp + k
            t = ct[yh, yl, l] + r2[0, l] + r2[1, l]
            for xx in range(NX):
                fo[lp, xx, k] = t[64 * xx:64 * xx + 64]
        for dx in range(1, NX):
            xx = up(x, dx, NX)
            fsend[lp, dx] = go(rcopy(fo.at[lp, xx], fi.at[lp, x], fs.at[lp, dx], fr.at[lp, dx], dev(xx, y, z, q)))
        fsend[lp, 0] = pltpu.make_async_copy(fo.at[lp, x], fi.at[lp, x], loc.at[lp])
        fsend[lp, 0].start()
    for lp in range(2):
        fsend[lp, 0].wait()
        for dx in range(1, NX):
            fsend[lp, dx].wait_recv()
        for k in range(2):
            for e in range(2):
                t = jnp.concatenate([fi[lp, xx, k, 32 * e:32 * e + 32] for xx in range(NX)], axis=0)
                out_ref[2 * lp + k, e] = t.T

    for c in started + [c for k in direct for c in k]:
        c.wait_send()

    @pl.when(q == 0)
    def _():
        for c in zd:
            c.wait_send()
        c3b.wait_send()

    @pl.when(q == 1)
    def _():
        c0.wait_send()


def on_device(p_vals, p_cols, out_cols):
    dma = pltpu.SemaphoreType.DMA
    vm = pltpu.VMEM
    return pl.pallas_call(
        kernel,
        out_shape=jax.ShapeDtypeStruct((4, 2, 128, 128), F32),
        in_specs=[pl.BlockSpec(memory_space=pltpu.VMEM)] * 3,
        out_specs=pl.BlockSpec(memory_space=pltpu.VMEM),
        scratch_shapes=[
            vm((4, 2, 128, 128), F32),
            vm((2, 4, 4, 4, 8, 128), F32),
            vm((8, 128), jnp.int32),
            vm((16, 8, 128), jnp.int32),
            pltpu.SMEM((16, 8, 128), jnp.int32),
            vm((128, 128), jnp.int32),
            pltpu.SMEM((128, 128), jnp.int32),
            vm((4, 4, 4, 2, 32, 128), F32),
            vm((2, 4, 2, 2, 8, 4, 8, 128), F32),
            vm((1025, 4, 8, 128), F32),
            vm((16, 8, 128), jnp.int32),
            vm((2, 512, 256), BF16),
            vm((2, 256, 256), BF16),
            vm((2, 2, 4, 256, 128), F32),
            vm((2, 2, 2, 128, 128), F32),
            vm((2, 4, 256, 128), F32),
            vm((2, 4, 2, 64, 128), F32),
            vm((2, 4, 2, 64, 128), F32),
            dma((2, 15)), dma((2, 15)), dma((5,)), dma((5,)), dma((4,)), dma((4,)), dma((2, 4)), dma((2, 4)), dma((4,)), dma((4,)),
            dma((4, 2)), dma((4, 2)), dma((5,)), dma((5,)), dma((2, 2)), dma((2, 2)), dma((2, 2, 2)), dma((2, 2, 2)),
            dma((2, 4)), dma((2, 4)), dma((4,)),
        ],
        compiler_params=pltpu.CompilerParams(collective_id=0, has_side_effects=True),
        name="square",
    )(p_vals, p_cols, out_cols)


def solution(mesh):
    placed = (P("row", "col", None, None), P("row", None), P("row", None))
    return jax.shard_map(
        on_device,
        mesh=mesh,
        in_specs=placed,
        out_specs=P("row", "col", None, None),
        check_vma=False,
    )
```

time: 639 us -> 76.5 us (0.12); the launches traced: 631 us -> 76.4 us
  waiting for transfers between devices: 477 us -> 0 us
  matrix products: 75.1 us -> 0 us
  Pallas kernels: 0 us -> 74.5 us
  starting transfers between devices: 34.4 us -> 0 us
  other arithmetic: 15.6 us -> 0 us
  between operations: 14.5 us -> 0.01 us
  local copies, waits for them, and re-layouts: 13.7 us -> 1.87 us
    ppermute x10 -> x0, waiting for transfers between devices: 308 us -> none  [from_behind(): return lax.ppermute(block, axis, route)]
    unnamed x3 -> x0, waiting for transfers between devices: 110 us -> none
    dot_general x6 -> x0, matrix products: 75.1 us -> none  [the longest x3 47.5 us: on_device(): jnp.einsum('isab,isobc->ioac', p_vals, mixed, precision=lax.Precision.HIG...]
    pallas_call x0 -> x1, Pallas kernels: none -> 74.5 us  [on_device(): pl.pallas_call(kernel, out_shape=jax.ShapeDtypeStruct((4, 2, 128, 128), F...]
    all_gather x1 -> x0, waiting for transfers between devices: 59.3 us -> none  [on_device(): panel_vals = lax.all_gather(p_vals, 'col', axis=1, tiled=True)]
    ppermute x10 -> x0, starting transfers between devices: 34.3 us -> none  [from_behind(): return lax.ppermute(block, axis, route)]
    select_n x6 -> x0, other arithmetic: 15.3 us -> none  [the longest x3 15.3 us: on_device(): panel_vals = jnp.where(taken, moved[0], panel_vals)]
    all_gather x1 -> x0, local copies, waits for them, and re-layouts: 6.59 us -> none  [on_device(): panel_vals = lax.all_gather(p_vals, 'col', axis=1, tiled=True)]
  transfers between devices with their start and end apart: 12 -> 0, of which waited for: 11 -> 0; matrix products, arithmetic and copies ran while one was open for 6% -> 0% of each run, Pallas kernels for 0% -> 0%
where the time goes in v3:
time: 76.5 us; the launch traced here: 76.4 us
  Pallas kernels  74.5 us (97%)
  local copies, waits for them, and re-layouts  1.87 us (2%)
    pallas_call x1, Pallas kernels, on_device(): pl.pallas_call(kernel, out_shape=jax.ShapeDtypeStruct((4, 2, 128, 128), F...  74.5 us
    unnamed x1, local copies, waits for them, and re-layouts  1.87 us

profile of v3, /device:TPU:1, one launch (start us, length us, event | category | flops | bytes accessed | tf_op | source)
XLA Modules:
  0.0 76.4 jit_solution(5044243398119922258)
XLA Ops:
  0.0 74.5 %square.1 = f32[4,2,128,128]{3,2,1,0:T(8,128)} custom-call(f32[4,2,128,128]{3,2,1,0:T(8,128)} %p_ref.1, s32[4,16]{1,0:T(4,128)} %pc_ref.1, s32[4,16]{1,0:T(4,128)} %oc_ref.1), custom_call_target="tpu_custom_call" | custom-call | tf_op jit(solution)/shard_map/square/pallas_call | solution.py:371
  74.5 1.9 %copy.5 = f32[4,2,128,128]{3,2,1,0:T(8,128)} copy(f32[4,2,128,128]{3,2,1,0:T(8,128)} %square.1) | data formatting | bytes 1048576

commit v4 on v3

--- a/solution.py
+++ b/solution.py
@@ -9,6 +9,7 @@
 F32 = jnp.float32
 BF16 = jnp.bfloat16
 NX, NY, NZ = 4, 4, 8
+WAY = (0, 1, 0, 1)
 
 
 def up(v, d, n):
@@ -123,6 +124,23 @@
     mc.start()
     mc.wait()
 
+    direct = [beside(ag.at[x, ys], ys) for ys in range(NY)]
+
+    def arrived(dy):
+        ys = up(y, dy, NY)
+        rcopy(rows_y, ag.at[x, ys], ays.at[0], ayr.at[ys], right).wait_recv()
+        for c in beside(ag.at[x, ys], ys):
+            c.start()
+
+    arrived(1)
+    arrived(3)
+    for c in b1:
+        c.wait_recv()
+    za1, zb1 = level1(1)
+    c1 = go(rcopy(bg.at[q, 1], bg.at[q, 1], cs.at[0], cr.at[0], mate))
+
+    arrived(2)
+
     def pick(i, carry):
         h, l, s4 = lax.div(i, 16), lax.rem(lax.div(i, 4), 4), lax.rem(i, 4)
         mine = q * 8 + 2 + h
@@ -146,21 +164,8 @@
     ic = pltpu.make_async_copy(ix, ixs, loc.at[0])
     ic.start()
 
-    for c in b1:
-        c.wait_recv()
-    za1, zb1 = level1(1)
-    c1 = go(rcopy(bg.at[q, 1], bg.at[q, 1], cs.at[0], cr.at[0], mate))
-
-    direct = [beside(ag.at[x, ys], ys) for ys in range(NY)]
-    for ys in range(NY):
-        @pl.when(y != ys)
-        def _(ys=ys):
-            rcopy(rows_y, ag.at[x, ys], ays.at[0], ayr.at[ys], right).wait_recv()
-            for c in direct[ys]:
-                c.start()
-
     def onward(ys):
-        n = ys % 2
+        n = WAY[ys]
         direct[ys][n].wait_recv()
         ref = ag.at[(xm, xp)[n], ys]
         return go(rcopy(ref, ref, afs.at[ys], afr.at[ys], (right, left)[n]))
@@ -210,7 +215,6 @@
     c1.wait_recv()
     both(1 - q, 1)
 
-    far = [onward(0), onward(1)]
     zc1 = level2(1, za1)
     zd = [rcopy(bg.at[0, 2, 1, e], bg.at[0, 3, 1, e], zs.at[3, e], zr.at[3, e], lower) for e in range(2)]
 
@@ -220,6 +224,7 @@
             c.start()
 
     c2 = go(rcopy(bg.at[q, 2], bg.at[q, 2], cs.at[1], cr.at[1], mate))
+    far = [onward(0), onward(1)]
     zb0.wait_recv()
     zb1.wait_recv()
     c0 = rcopy(bg.at[1, 0, 1], bg.at[1, 0, 1], cs.at[4], cr.at[4], mate)
@@ -262,7 +267,7 @@
 
     def early(h):
         for ys in (2 * h, 2 * h + 1):
-            direct[ys][1 - ys % 2].wait_recv()
+            direct[ys][1 - WAY[ys]].wait_recv()
             far[ys].wait_recv()
         for s4 in range(2):
             def step(i, carry, s4=s4):
@@ -278,13 +283,13 @@
     c3a = go(rcopy(bg.at[q, 3, 0], bg.at[q, 3, 0], cs.at[2], cr.at[2], mate))
     c3b = rcopy(bg.at[0, 3, 1], bg.at[0, 3, 1], cs.at[3], cr.at[3], mate)
     expand(q, 3, 0)
-    early(1)
-
     @pl.when(q == 0)
     def _():
         for c in zd:
             c.wait_recv()
         c3b.start()
+
+    early(1)
 
     c3a.wait_recv()
     expand(1 - q, 3, 0)

time: 76.5 us -> 73.7 us (0.963)
  Pallas kernels: 74.5 us -> 71.6 us
    pallas_call x1, Pallas kernels: 74.5 us -> 71.6 us  [on_device(): pl.pallas_call(kernel, out_shape=jax.ShapeDtypeStruct((4, 2, 128, 128), F...]
where the time goes in v4:
time: 73.7 us; the launch traced here: 73.5 us
  Pallas kernels  71.6 us (97%)
  local copies, waits for them, and re-layouts  1.87 us (3%)
    pallas_call x1, Pallas kernels, on_device(): pl.pallas_call(kernel, out_shape=jax.ShapeDtypeStruct((4, 2, 128, 128), F...  71.6 us
    unnamed x1, local copies, waits for them, and re-layouts  1.87 us

profile of v4, /device:TPU:1, one launch (start us, length us, event | category | flops | bytes accessed | tf_op | source)
XLA Modules:
  0.0 73.5 jit_solution(9337725249552666176)
XLA Ops:
  0.0 71.6 %square.1 = f32[4,2,128,128]{3,2,1,0:T(8,128)} custom-call(f32[4,2,128,128]{3,2,1,0:T(8,128)} %p_ref.1, s32[4,16]{1,0:T(4,128)} %pc_ref.1, s32[4,16]{1,0:T(4,128)} %oc_ref.1), custom_call_target="tpu_custom_call" | custom-call | tf_op jit(solution)/shard_map/square/pallas_call | solution.py:376
  71.6 1.9 %copy.5 = f32[4,2,128,128]{3,2,1,0:T(8,128)} copy(f32[4,2,128,128]{3,2,1,0:T(8,128)} %square.1) | data formatting | bytes 1048576
